TPU v7x, 32 devices: a whole 2x2x4 slice. The times are simulated.
32 devices in a mesh: span: 8 (over z, x), chord: 4 (over y, core).
Axes of the slice: x: 2, y: 2, z: 4, core: 2. Of those that a mesh axis runs over, the one named last changes fastest.
Arguments:
- pressure: float32 [2, 1024, 512], P(None, 'span', 'chord'), may hold values from 0 to 1
- fill_state: int32 [2, 1024, 512], P(None, 'span', 'chord'), may hold values from 0 to 2
- perm_class: int32 [2, 1024, 512], P(None, 'span', 'chord'), may hold values from 0 to 7
- perm_table: float32 [2, 8], replicated, may hold values from 1 to 4
- inlet_span: int32 [128], replicated, may hold values from 0 to 1023
- inlet_chord: int32 [128], replicated, may hold values from 0 to 511
- inlet_rate: float32 [128], replicated, may hold values from 500 to 1500
Outputs:
- pressure_out: float32 [2, 1024, 512], P(None, 'span', 'chord')
Inputs may be any that keep to these rules, and one draw needn't show every extreme that they name: `inlet_span`: inlet cells may repeat; their rates add.
All inputs are finite; a program needn't handle non-finite values.
Results may differ from a plain program's by a relative error of at most 0.00035.
Values sent between devices are 32-bit elements; how exact they have to be, the bound alone decides.
A program may use at most 64 MiB of HBM per device.

v0:
```python
import jax
import jax.numpy as jnp
from jax import lax
from jax.sharding import PartitionSpec as P

HALF_RATE = 200.0
COUPLE = 0.3


def shift_lower(values, stride):
    padding = jnp.zeros(values.shape[:-1] + (stride,), values.dtype)
    return jnp.concatenate([padding, values[..., :-stride]], axis=-1)


def shift_upper(values, stride):
    padding = jnp.zeros(values.shape[:-1] + (stride,), values.dtype)
    return jnp.concatenate([values[..., stride:], padding], axis=-1)


def faces(cond):
    summed = HALF_RATE * (cond + shift_upper(cond, 1))
    closing = jnp.zeros(cond.shape[:-1] + (1,), cond.dtype)
    return jnp.concatenate([summed[..., :-1], closing], axis=-1)


def parallel_cyclic_reduction_update(
    lower_band,
    diagonal_terms,
    upper_band,
    right_hand_side,
    previous_neighbour_row,
    next_neighbour_row,
):
    new_lower = -lower_band * previous_neighbour_row[0]
    new_diag = (
        diagonal_terms - lower_band * previous_neighbour_row[1] - upper_band * next_neighbour_row[0]
    )
    new_upper = -upper_band * next_neighbour_row[1]
    new_rhs = (
        right_hand_side
        - lower_band * previous_neighbour_row[2]
        - upper_band * next_neighbour_row[2]
    )
    return (new_lower, new_diag, new_upper, new_rhs)


def line_solve(lower_band, diagonal_terms, upper_band, right_hand_side):
    total = right_hand_side.shape[-1]
    stride = 1
    while stride < total:
        ratios = (
            lower_band / diagonal_terms,
            upper_band / diagonal_terms,
            right_hand_side / diagonal_terms,
        )
        previous_neighbour_row = [shift_lower(v, stride) for v in ratios]
        next_neighbour_row = [shift_upper(v, stride) for v in ratios]
        lower_band, diagonal_terms, upper_band, right_hand_side = parallel_cyclic_reduction_update(
            lower_band,
            diagonal_terms,
            upper_band,
            right_hand_side,
            previous_neighbour_row,
            next_neighbour_row,
        )
        stride = stride * 2
    return right_hand_side / diagonal_terms


def explicit_core(field, field_next, field_prev, faces_here, faces_prev, source):
    flux = faces_here * (field_next - field) - faces_prev * (field - field_prev)
    return field + flux + COUPLE * (jnp.flip(field, 0) - field) + source


def explicit_lines(field, faces_here, faces_prev, source):
    return explicit_core(
        field, shift_upper(field, 1), shift_lower(field, 1), faces_here, faces_prev, source
    )


def second_half(star, half_lines, source):
    return 2.0 * star - half_lines + COUPLE * (jnp.flip(star, 0) - star) + source


def to_span(block):
    turned = jnp.transpose(block, (0, 2, 1))
    return lax.all_to_all(turned, "span", split_axis=1, concat_axis=2, tiled=True)


def span_return(lines):
    turned = lax.all_to_all(lines, "span", split_axis=2, concat_axis=1, tiled=True)
    return jnp.transpose(turned, (0, 2, 1))


def to_chord(block):
    return lax.all_to_all(block, "chord", split_axis=1, concat_axis=2, tiled=True)


def from_chord(lines):
    return lax.all_to_all(lines, "chord", split_axis=2, concat_axis=1, tiled=True)


def per_device(pressure, fill_state, perm_class, perm_table, inlet_span, inlet_chord, inlet_rate):
    plies = pressure.shape[0]
    rows = pressure.shape[1]
    width = pressure.shape[2]
    mobility = jnp.where(fill_state == 0, 1.0, jnp.where(fill_state == 1, 0.5, 0.25))
    perm = jnp.zeros(pressure.shape, jnp.float32)
    for klass in range(perm_table.shape[1]):
        perm = perm + jnp.where(perm_class == klass, perm_table[:, klass][:, None, None], 0.0)
    cond = perm * mobility
    row_global = lax.axis_index("span") * rows + jnp.arange(rows, dtype=jnp.int32)
    col_global = lax.axis_index("chord") * width + jnp.arange(width, dtype=jnp.int32)
    row_hits = (row_global[:, None] == inlet_span[None, :]).astype(jnp.float32) * inlet_rate[
        None, :
    ]
    col_hits = (inlet_chord[:, None] == col_global[None, :]).astype(jnp.float32)
    plane = jnp.dot(
        row_hits, col_hits, precision=lax.Precision.HIGHEST, preferred_element_type=jnp.float32
    )
    source = plane[None]
    span_setup = to_span(jnp.concatenate([cond, source], axis=0))
    span_faces = faces(span_setup[:plies])
    span_prev = shift_lower(span_faces, 1)
    span_source = span_setup[plies:]
    span_diag = 1.0 + span_prev + span_faces
    chord_setup = to_chord(jnp.concatenate([cond, source, pressure], axis=0))
    chord_faces = faces(chord_setup[:plies])
    chord_prev = shift_lower(chord_faces, 1)
    chord_diag = 1.0 + chord_prev + chord_faces
    chord_source = chord_setup[plies : plies + 1]
    field = chord_setup[plies + 1 :]
    half = explicit_lines(field, chord_faces, chord_prev, chord_source)
    half_lines = to_span(from_chord(half))
    star = line_solve(-span_prev, span_diag, -span_faces, half_lines)
    second = second_half(star, half_lines, span_source)
    returned = to_chord(span_return(second))
    field = line_solve(-chord_prev, chord_diag, -chord_faces, returned)
    result = from_chord(field)
    return result


def solution(mesh):
    placed = (
        P(None, "span", "chord"),
        P(None, "span", "chord"),
        P(None, "span", "chord"),
        P(),
        P(),
        P(),
        P(),
    )
    return jax.shard_map(
        per_device, mesh=mesh, in_specs=placed, out_specs=P(None, "span", "chord"), check_vma=False
    )
```

profile of v0, /device:TPU:0, one launch (start us, length us, event | category | flops | bytes accessed | tf_op | source)
XLA Modules:
  0.0 96.3 jit_solution(14580648930356081755)
XLA Ops:
  0.0 0.7 copy-done.2
  0.7 0.3 slice_reduce_fusion.7
  1.0 1.0 %copy.86 = f32[2,128,128]{2,0,1:T(2,128)S(1)} copy(f32[2,128,128]{2,1,0:T(8,128)} %param.7) | data formatting | bytes 262144 | tf_op args[0]
  2.1 0.2 fusion.16
  2.4 0.6 copy-done
  3.0 0.6 fusion.13
  3.5 1.0 %pad_maximum_fusion = f32[5,128,128]{2,0,1:T(8,128)} fusion(f32[2,128,128]{2,0,1:T(2,128)S(1)} %copy.86, f32[1,128,128]{2,0,1:T(1,128)S(1)} %bitcast.122, f32[2,128,128]{2,0,1:T(2,128)S(1)} %fusion.13), kind=kLoop, calls=%fused_computation | loop fusion | flops 163840 | bytes 655360 | tf_op jit(solution)/shard_map/concatenate | solution.py:127
  4.5 4.3 %all-to-all-start = ((f32[5,128,128]{2,0,1:T(8,128)}), f32[5,128,128]{2,0,1:T(8,128)S(1)}, u32[]{:S(2)}, u32[]{:S(2)}) async-start(f32[5,128,128]{2,0,1:T(8,128)} %pad_maximum_fusion), calls=%async_computation | async-start | bytes 1048576 | tf_op jit(solution)/shard_map/all_to_all | solution.py:96
  8.9 0.9 copy.98
  9.8 7.8 %all-to-all-done = f32[5,128,128]{2,0,1:T(8,128)S(1)} async-done(((f32[5,128,128]{2,0,1:T(8,128)}), f32[5,128,128]{2,0,1:T(8,128)S(1)}, u32[]{:S(2)}, u32[]{:S(2)}) %all-to-all-start) | async-done | bytes 327712 | tf_op jit(solution)/shard_map/all_to_all | solution.py:96
  17.6 6.5 %all-to-all-start.3 = ((f32[3,128,128]{2,0,1:T(4,128)}), f32[3,128,128]{2,0,1:T(4,128)S(1)}, u32[]{:S(2)}, u32[]{:S(2)}) async-start(f32[3,128,128]{2,0,1:T(4,128)} %copy.98), calls=%async_computation.3 | async-start | bytes 524288 | tf_op jit(solution)/shard_map/all_to_all | solution.py:87
  24.5 0.6 copy-done.4
  25.2 0.1 fusion.2
  25.3 0.2 copy.91
  25.6 1.2 %reshape.34 = f32[4,1,8192]{2,1,0:T(1,128)} reshape(f32[512,2,32]{2,1,0:T(2,128)S(1)} %bitcast.97) | data formatting | bytes 262144
  26.8 5.9 %all-to-all-done.3 = f32[3,128,128]{2,0,1:T(4,128)S(1)} async-done(((f32[3,128,128]{2,0,1:T(4,128)}), f32[3,128,128]{2,0,1:T(4,128)S(1)}, u32[]{:S(2)}, u32[]{:S(2)}) %all-to-all-start.3) | async-done | bytes 196640 | tf_op jit(solution)/shard_map/all_to_all | solution.py:87
  32.7 3.3 %all-to-all-start.1 = ((f32[4,1,8192]{2,1,0:T(1,128)}), f32[4,1,8192]{2,1,0:T(1,128)S(1)}, u32[]{:S(2)}, u32[]{:S(2)}) async-start(f32[4,1,8192]{2,1,0:T(1,128)} %reshape.34), calls=%async_computation.1 | async-start | bytes 262144 | tf_op jit(solution)/shard_map/all_to_all | solution.py:100
  36.2 4.4 %all-to-all-done.1 = f32[4,1,8192]{2,1,0:T(1,128)S(1)} async-done(((f32[4,1,8192]{2,1,0:T(1,128)}), f32[4,1,8192]{2,1,0:T(1,128)S(1)}, u32[]{:S(2)}, u32[]{:S(2)}) %all-to-all-start.1) | async-done | bytes 131104 | tf_op jit(solution)/shard_map/all_to_all | solution.py:100
  40.6 0.6 broadcast.342
  41.2 1.0 %reduce.16 = f32[4,8192]{1,0:T(4,128)S(1)} reduce(f32[4,1,8192]{2,1,0:T(1,128)S(1)} %all-to-all-done.1, f32[]{:T(128)} %broadcast.342), dimensions={1}, to_apply=%all_to_all.90.reduce_sub_computation | reduce | bytes 262148 | tf_op jit(solution)/shard_map/all_to_all | solution.py:100
  42.2 0.5 reshape.35
  42.7 0.2 copy.111
  42.9 0.8 copy.94
  43.6 3.6 %all-to-all-start.2 = ((f32[2,128,128]{2,0,1:T(2,128)}), f32[2,128,128]{2,0,1:T(2,128)S(1)}, u32[]{:S(2)}, u32[]{:S(2)}) async-start(f32[2,128,128]{2,0,1:T(2,128)} %copy.94), calls=%async_computation.2 | async-start | bytes 262144 | tf_op jit(solution)/shard_map/all_to_all | solution.py:87
  47.2 7.3 %all-to-all-done.2 = f32[2,128,128]{2,0,1:T(2,128)S(1)} async-done(((f32[2,128,128]{2,0,1:T(2,128)}), f32[2,128,128]{2,0,1:T(2,128)S(1)}, u32[]{:S(2)}, u32[]{:S(2)}) %all-to-all-start.2) | async-done | bytes 131104 | tf_op jit(solution)/shard_map/all_to_all | solution.py:87
  54.6 0.7 copy-done.3
  55.7 0.2 fusion.44
  55.9 0.1 fusion.60
  56.3 0.1 fusion.43
  56.9 0.1 fusion.42
  58.0 0.1 fusion.40
  58.6 0.1 fusion.39
  59.2 0.1 fusion.38
  60.0 0.5 copy.102
  60.5 1.4 %reshape.36 = f32[8,1,4096]{2,1,0:T(1,128)S(1)} reshape(f32[1024,2,16]{2,1,0:T(2,128)S(1)} %bitcast.95) | data formatting | bytes 262144
  62.0 9.7 %all_to_all.120 = f32[8,1,4096]{2,1,0:T(1,128)S(1)} all-to-all(f32[8,1,4096]{2,1,0:T(1,128)S(1)} %reshape.36), channel_id=1, replica_groups=mesh['span'=8,'chord'=4] {'span'}, dimensions={0} | all-to-all | bytes 262144 | tf_op jit(solution)/shard_map/all_to_all | solution.py:91
  71.7 1.0 %reduce.17 = f32[8,4096]{1,0:T(8,128)S(1)} reduce(f32[8,1,4096]{2,1,0:T(1,128)S(1)} %all_to_all.120, f32[]{:T(128)} %broadcast.342), dimensions={1}, to_apply=%all_to_all.101.reduce_sub_computation | reduce | bytes 262148 | tf_op jit(solution)/shard_map/all_to_all | solution.py:91
  72.7 1.4 %reshape.37 = f32[1024,2,16]{2,1,0:T(2,128)S(1)} reshape(f32[8,4096]{1,0:T(8,128)S(1)} %reduce.17) | data formatting | bytes 262144
  74.1 0.4 copy.113
  74.6 7.0 %all_to_all.121 = f32[2,128,128]{2,0,1:T(2,128)S(1)} all-to-all(f32[2,128,128]{2,0,1:T(2,128)S(1)} %copy.105), channel_id=1, replica_groups=mesh['span'=8,'chord'=4] {'chord'}, dimensions={1} | all-to-all | bytes 262144 | tf_op jit(solution)/shard_map/all_to_all | solution.py:96
  82.1 0.2 fusion.34
  86.2 0.2 copy.108
  86.4 0.5 reshape.38
  87.0 7.0 %all_to_all.122 = f32[4,1,8192]{2,1,0:T(1,128)S(1)} all-to-all(f32[4,1,8192]{2,1,0:T(1,128)S(1)} %reshape.38), channel_id=1, replica_groups=mesh['span'=8,'chord'=4] {'chord'}, dimensions={0} | all-to-all | bytes 262144 | tf_op jit(solution)/shard_map/all_to_all | solution.py:100
  94.0 1.0 %reduce.18 = f32[4,8192]{1,0:T(4,128)S(1)} reduce(f32[4,1,8192]{2,1,0:T(1,128)S(1)} %all_to_all.122, f32[]{:T(128)} %broadcast.342), dimensions={1}, to_apply=%all_to_all.109.reduce_sub_computation | reduce | bytes 262148 | tf_op jit(solution)/shard_map/all_to_all | solution.py:100
  95.0 0.5 reshape.39
  95.5 0.2 copy.114
  95.7 0.7 copy.110
  (119 shorter events, 8.2 us)
Async XLA Ops:
  0.0 0.7 copy-start.2
  1.0 1.1 %copy-start.5 = (f32[128]{0:T(128)S(1)}, f32[128]{0:T(128)}, u32[]{:S(2)}) copy-start(f32[128]{0:T(128)} %param.13) | copy-start | bytes 1540
  1.0 1.1 %copy-start.6 = (s32[128]{0:T(128)S(1)}, s32[128]{0:T(128)}, u32[]{:S(2)}) copy-start(s32[128]{0:T(128)} %param.11) | copy-start | bytes 1540
  1.0 1.1 %copy-start.7 = (s32[128]{0:T(128)S(1)}, s32[128]{0:T(128)}, u32[]{:S(2)}) copy-start(s32[128]{0:T(128)} %param.12) | copy-start | bytes 1540
  1.0 1.4 %copy-start.1 = (s32[2,128,128]{2,1,0:T(8,128)S(1)}, s32[2,128,128]{2,1,0:T(8,128)}, u32[]{:S(2)}) copy-start(s32[2,128,128]{2,1,0:T(8,128)} %param.9) | copy-start | bytes 393220
  2.1 0.9 copy-start
  4.5 13.1 %all-to-all-start = ((f32[5,128,128]{2,0,1:T(8,128)}), f32[5,128,128]{2,0,1:T(8,128)S(1)}, u32[]{:S(2)}, u32[]{:S(2)}) async-start(f32[5,128,128]{2,0,1:T(8,128)} %pad_maximum_fusion), calls=%async_computation | async-start | bytes 1048576 | tf_op jit(solution)/shard_map/all_to_all | solution.py:96
  17.6 15.1 %all-to-all-start.3 = ((f32[3,128,128]{2,0,1:T(4,128)}), f32[3,128,128]{2,0,1:T(4,128)S(1)}, u32[]{:S(2)}, u32[]{:S(2)}) async-start(f32[3,128,128]{2,0,1:T(4,128)} %copy.98), calls=%async_computation.3 | async-start | bytes 524288 | tf_op jit(solution)/shard_map/all_to_all | solution.py:87
  24.5 0.7 copy-start.4
  32.7 7.9 %all-to-all-start.1 = ((f32[4,1,8192]{2,1,0:T(1,128)}), f32[4,1,8192]{2,1,0:T(1,128)S(1)}, u32[]{:S(2)}, u32[]{:S(2)}) async-start(f32[4,1,8192]{2,1,0:T(1,128)} %reshape.34), calls=%async_computation.1 | async-start | bytes 262144 | tf_op jit(solution)/shard_map/all_to_all | solution.py:100
  43.6 10.9 %all-to-all-start.2 = ((f32[2,128,128]{2,0,1:T(2,128)}), f32[2,128,128]{2,0,1:T(2,128)S(1)}, u32[]{:S(2)}, u32[]{:S(2)}) async-start(f32[2,128,128]{2,0,1:T(2,128)} %copy.94), calls=%async_computation.2 | async-start | bytes 262144 | tf_op jit(solution)/shard_map/all_to_all | solution.py:87
  54.6 0.7 copy-start.3
where the time goes:
time: 97 us; the launch traced here: 96.3 us
  waiting for transfers between devices  25.4 us (26%)
  blocking collectives  23.7 us (24%)
  local copies, waits for them, and re-layouts  18.9 us (19%)
  starting transfers between devices  17.6 us (18%)
  other arithmetic  9.41 us (10%)
  between operations  0.99 us (1%)
    all_to_all x2, waiting for transfers between devices, to_span(): lax.all_to_all(turned, 'span', split_axis=1, concat_axis=2, tiled=True)  13.2 us
    all_to_all x2, starting transfers between devices, to_span(): lax.all_to_all(turned, 'span', split_axis=1, concat_axis=2, tiled=True)  10 us
    all_to_all x1, blocking collectives, span_return(): lax.all_to_all(lines, 'span', split_axis=2, concat_axis=1, tiled=True)  9.74 us
    unnamed x26, local copies, waits for them, and re-layouts  9.18 us
    all_to_all x1, waiting for transfers between devices, to_chord(): lax.all_to_all(block, 'chord', split_axis=1, concat_axis=2, tiled=True)  7.84 us
    all_to_all x1, blocking collectives, to_chord(): lax.all_to_all(block, 'chord', split_axis=1, concat_axis=2, tiled=True)  6.99 us
    all_to_all x1, blocking collectives, from_chord(): lax.all_to_all(lines, 'chord', split_axis=2, concat_axis=1, tiled=True)  6.99 us
    all_to_all x1, waiting for transfers between devices, from_chord(): lax.all_to_all(lines, 'chord', split_axis=2, concat_axis=1, tiled=True)  4.36 us
  transfers between devices with their start and end apart: 4, of which 4 were waited for; matrix products, arithmetic and copies ran while one was open for 3% of the time, Pallas kernels for 0%

commit v1 on v0

v1 whole, which is shorter than its diff:
```python
import functools

import jax
import jax.numpy as jnp
from jax import lax
from jax.experimental import pallas as pl
from jax.experimental.pallas import tpu as pltpu
from jax.sharding import PartitionSpec as P

HALF_RATE = 200.0
COUPLE = 0.3
MESH = pl.DeviceIdType.MESH
TILE = 8


def down(x, s):
    if s % TILE == 0:
        return jnp.concatenate([x[-s:], x[:-s]], axis=0)
    return pltpu.roll(x, s, 0)


def up(x, s):
    if s % TILE == 0:
        return jnp.concatenate([x[s:], x[:s]], axis=0)
    return pltpu.roll(x, x.shape[0] - s, 0)


def from_row(s, value, other):
    if s % TILE == 0:
        return jnp.concatenate([other[:s], value[s:]], axis=0)
    rows = lax.broadcasted_iota(jnp.int32, value.shape, 0)
    return jnp.where(rows >= s, value, other)


def to_row(s, value, other):
    n = value.shape[0]
    if s % TILE == 0:
        return jnp.concatenate([value[: n - s], other[n - s :]], axis=0)
    rows = lax.broadcasted_iota(jnp.int32, value.shape, 0)
    return jnp.where(rows < n - s, value, other)


def factor(cond, keep):
    n = cond.shape[0]
    zero = jnp.zeros_like(cond)
    one = jnp.ones_like(cond)
    g = HALF_RATE * (cond + up(cond, 1))
    a = from_row(1, down(g, 1), one)
    c = to_row(1, g, one)
    e = one
    s, k = 1, 0
    while s < n:
        a_in = from_row(s, a, zero)
        c_in = to_row(s, c, zero)
        rb = 1.0 / (e + a_in + c_in)
        al = a_in * down(rb, s)
        be = c_in * up(rb, s)
        keep(k, al, be)
        a = from_row(s, al * down(a, s), a)
        c = to_row(s, be * up(c, s), c)
        e = e + al * down(e, s) + be * up(e, s)
        s, k = 2 * s, k + 1
    re = 1.0 / e
    return a * re, c * re, re


def reduce_rhs(d, kept, re):
    n = d.shape[0]
    s, k = 1, 0
    while s < n:
        al, be = kept(k)
        if s % TILE == 0:
            zero = jnp.zeros_like(d[:s])
            d = (
                d
                + jnp.concatenate([zero, al[s:] * d[:-s]], axis=0)
                + jnp.concatenate([be[:-s] * d[s:], zero], axis=0)
            )
        else:
            d = d + al * down(d, s) + be * up(d, s)
        s, k = 2 * s, k + 1
    return d * re


class Gather:
    def __init__(self, axis, n, me, buf, send, recv):
        self.copies = []
        self.landed = []
        for o in range(1, n):
            dst = lax.rem(me + o, n)
            src = lax.rem(me + n - o, n)
            self.copies.append(
                pltpu.make_async_remote_copy(
                    buf.at[me], buf.at[me], send.at[o], recv.at[o], {axis: dst}, MESH
                )
            )
            self.landed.append(
                pltpu.make_async_remote_copy(
                    buf.at[src], buf.at[src], send.at[o], recv.at[o], {axis: dst}, MESH
                )
            )

    def start(self):
        for copy in self.copies:
            copy.start()

    def wait(self):
        for copy in self.landed:
            copy.wait_recv()

    def wait_sent(self):
        for copy in self.copies:
            copy.wait_send()


def put_coefs(buf, me, plies, p, A, C, cond):
    n = A.shape[0]
    values = (A[:1], C[n - 1 :], A[n - 1 :], cond[:1], cond[n - 1 :])
    for q, v in enumerate(values):
        buf[me, q * plies + p : q * plies + p + 1, :] = v


def flux_factor(buf, n, plies):
    def at(j, q):
        return buf[j, q * plies : (q + 1) * plies, :]

    w, m = [None] * (n + 1), [None] * (n + 1)
    cross = [at(j, 2) for j in range(n)]
    for j in range(1, n):
        diag = 1.0 / (HALF_RATE * (at(j - 1, 4) + at(j, 3))) + at(j - 1, 1) + at(j, 0)
        if j > 1:
            m[j] = cross[j - 1] * w[j - 1]
            diag = diag - cross[j - 1] * m[j]
        w[j] = 1.0 / diag
    return w, m, cross


def flux_solve(buf, n, plies, me, w, m, cross):
    y = [None] * (n + 1)
    for j in range(1, n):
        r = buf[j - 1, plies : 2 * plies, :] - buf[j, :plies, :]
        y[j] = r if j == 1 else r + m[j] * y[j - 1]
    zero = jnp.zeros((plies, buf.shape[-1]), jnp.float32)
    top, bottom = zero, zero
    flux = None
    for j in range(n - 1, 0, -1):
        flux = w[j] * (y[j] if flux is None else y[j] + cross[j] * flux)
        top = jnp.where(me == j, flux, top)
        bottom = jnp.where(me + 1 == j, flux, bottom)
    return top, bottom


def kernel(
    ns, nc, plies, classes,
    pressure_hbm, fill_hbm, class_hbm, table_ref, span_ref, chord_ref, rate_ref,
    out_ref,
    pressure, fill, klass, half, keep_s, keep_c, A_s, C_s, E_s, A_c, C_c, E_c, D,
    halo_out, halo_in, coef_s, coef_c, edge_s, edge_c,
    load_sem, halo_send, halo_recv,
    cs_send, cs_recv, cc_send, cc_recv, es_send, es_recv, ec_send, ec_recv,
):
    rows, width = pressure.shape[1:]
    me_s, me_c = lax.axis_index("span"), lax.axis_index("chord")
    barrier = pltpu.get_barrier_semaphore()
    for o in range(1, nc):
        pl.semaphore_signal(
            barrier, inc=1, device_id={"chord": lax.rem(me_c + o, nc)}, device_id_type=MESH
        )
    for o in range(1, ns):
        pl.semaphore_signal(
            barrier, inc=1, device_id={"span": lax.rem(me_s + o, ns)}, device_id_type=MESH
        )
    loads = [
        pltpu.make_async_copy(src, dst, load_sem.at[i])
        for i, (src, dst) in enumerate(
            ((class_hbm, klass), (fill_hbm, fill), (pressure_hbm, pressure))
        )
    ]
    for load in loads:
        load.start()

    row_id = lax.broadcasted_iota(jnp.int32, (rows, span_ref.shape[1]), 0) + me_s * rows
    col_id = lax.broadcasted_iota(jnp.int32, (width, span_ref.shape[1]), 0) + me_c * width
    row_hits = jnp.where(row_id == span_ref[...], rate_ref[...], 0.0)
    col_hits = jnp.where(col_id == chord_ref[...], 1.0, 0.0)
    plane = lax.dot_general(
        row_hits, col_hits, (((1,), (1,)), ((), ())),
        precision=lax.Precision.HIGHEST, preferred_element_type=jnp.float32,
    )

    for load in loads:
        load.wait()

    conds, turned, fields = [], [], []
    for p in range(plies):
        perm = jnp.full((rows, width), table_ref[p, 0], jnp.float32)
        kl = klass[p]
        for k in range(1, classes):
            perm = jnp.where(kl == k, table_ref[p, k], perm)
        st = fill[p]
        cond = perm * jnp.where(st == 0, 1.0, jnp.where(st == 1, 0.5, 0.25))
        conds.append(cond)
        turned.append(cond.T)
        fields.append(pressure[p].T)
        for side, at in ((0, 0), (1, width - 1)):
            halo_out[side, p : p + 1, :] = turned[p][at : at + 1]
            halo_out[side, plies + p : plies + p + 1, :] = fields[p][at : at + 1]

    pl.semaphore_wait(barrier, ns + nc - 2)
    ahead, behind = lax.rem(me_c + 1, nc), lax.rem(me_c + nc - 1, nc)
    halos = [
        pltpu.make_async_remote_copy(
            halo_out.at[side], halo_in.at[side], halo_send.at[side], halo_recv.at[side],
            {"chord": to}, MESH,
        )
        for side, to in ((0, behind), (1, ahead))
    ]
    for copy in halos:
        copy.start()

    def keeper(ref, p):
        def keep(k, al, be):
            ref[k, 0, p] = al
            ref[k, 1, p] = be

        return keep

    def kept(ref, p):
        return lambda k: (ref[k, 0, p], ref[k, 1, p])

    for p in range(plies):
        A, C, re = factor(conds[p], keeper(keep_s, p))
        A_s[p], C_s[p], E_s[p] = A, C, re
        put_coefs(coef_s, me_s, plies, p, A, C, conds[p])
    span_coefs = Gather("span", ns, me_s, coef_s, cs_send, cs_recv)
    span_coefs.start()

    explicit = []
    for p in range(plies):
        f, other = fields[p], fields[plies - 1 - p]
        g = HALF_RATE * (turned[p] + up(turned[p], 1))
        flow = to_row(1, g * (up(f, 1) - f), jnp.zeros_like(f))
        back = from_row(1, down(flow, 1), jnp.zeros_like(f))
        explicit.append(f + (flow - back) + COUPLE * (other - f))

    for copy in halos:
        copy.wait_recv()
    lanes = lax.broadcasted_iota(jnp.int32, (width, rows), 0)
    for p in range(plies):
        behind_c, behind_f = halo_in[1, p : p + 1, :], halo_in[1, plies + p : plies + p + 1, :]
        ahead_c, ahead_f = halo_in[0, p : p + 1, :], halo_in[0, plies + p : plies + p + 1, :]
        first = HALF_RATE * (behind_c + turned[p][:1]) * (behind_f - fields[p][:1])
        last = HALF_RATE * (ahead_c + turned[p][width - 1 :]) * (ahead_f - fields[p][width - 1 :])
        first = jnp.where(me_c > 0, first, 0.0)
        last = jnp.where(me_c < nc - 1, last, 0.0)
        total = (
            explicit[p]
            + jnp.where(lanes == 0, first, 0.0)
            + jnp.where(lanes == width - 1, last, 0.0)
        )
        rhs = total.T + plane
        half[p] = rhs
        d = reduce_rhs(rhs, kept(keep_s, p), E_s[p])
        D[p] = d
        edge_s[me_s, p : p + 1, :] = d[:1]
        edge_s[me_s, plies + p : plies + p + 1, :] = d[rows - 1 :]
    span_edges = Gather("span", ns, me_s, edge_s, es_send, es_recv)
    span_edges.start()

    for p in range(plies):
        A, C, re = factor(turned[p], keeper(keep_c, p))
        A_c[p], C_c[p], E_c[p] = A, C, re
        put_coefs(coef_c, me_c, plies, p, A, C, turned[p])
    chord_coefs = Gather("chord", nc, me_c, coef_c, cc_send, cc_recv)
    chord_coefs.start()

    span_coefs.wait()
    parts = flux_factor(coef_s, ns, plies)
    span_edges.wait()
    top, bottom = flux_solve(edge_s, ns, plies, me_s, *parts)
    stars = [D[p] + A_s[p] * top[p : p + 1] - C_s[p] * bottom[p : p + 1] for p in range(plies)]
    for p in range(plies):
        star, other = stars[p], stars[plies - 1 - p]
        second = 2.0 * star - half[p] + COUPLE * (other - star) + plane
        d = reduce_rhs(second.T, kept(keep_c, p), E_c[p])
        D[p] = d
        edge_c[me_c, p : p + 1, :] = d[:1]
        edge_c[me_c, plies + p : plies + p + 1, :] = d[width - 1 :]
    chord_edges = Gather("chord", nc, me_c, edge_c, ec_send, ec_recv)
    chord_edges.start()

    chord_coefs.wait()
    parts = flux_factor(coef_c, nc, plies)
    chord_edges.wait()
    top, bottom = flux_solve(edge_c, nc, plies, me_c, *parts)
    for p in range(plies):
        line = D[p] + A_c[p] * top[p : p + 1] - C_c[p] * bottom[p : p + 1]
        out_ref[p] = line.T

    for copy in halos:
        copy.wait_send()
    for gather in (span_coefs, chord_coefs, span_edges, chord_edges):
        gather.wait_sent()


def levels(n):
    return max(1, (n - 1).bit_length())


def per_device(ns, nc, pressure, fill_state, perm_class, perm_table, inlet_span, inlet_chord, inlet_rate):
    plies, rows, width = pressure.shape
    classes = perm_table.shape[1]
    inlets = inlet_span.shape[0]
    vmem = pl.BlockSpec(memory_space=pltpu.VMEM)
    hbm = pl.BlockSpec(memory_space=pl.ANY)
    smem = pl.BlockSpec(memory_space=pltpu.SMEM)
    f32 = jnp.float32
    block = pltpu.VMEM((plies, rows, width), f32)
    block_t = pltpu.VMEM((plies, width, rows), f32)
    iblock = pltpu.VMEM((plies, rows, width), jnp.int32)
    pad = lambda n: -(-n // TILE) * TILE
    dma = lambda n: pltpu.SemaphoreType.DMA((n,))
    return pl.pallas_call(
        functools.partial(kernel, ns, nc, plies, classes),
        out_shape=jax.ShapeDtypeStruct(pressure.shape, f32),
        in_specs=[hbm, hbm, hbm, smem, vmem, vmem, vmem],
        out_specs=vmem,
        scratch_shapes=[
            block, iblock, iblock, block,
            pltpu.VMEM((levels(rows), 2, plies, rows, width), f32),
            pltpu.VMEM((levels(width), 2, plies, width, rows), f32),
            block, block, block, block_t, block_t, block_t, block,
            pltpu.VMEM((2, pad(2 * plies), rows), f32),
            pltpu.VMEM((2, pad(2 * plies), rows), f32),
            pltpu.VMEM((ns, pad(5 * plies), width), f32),
            pltpu.VMEM((nc, pad(5 * plies), rows), f32),
            pltpu.VMEM((ns, pad(2 * plies), width), f32),
            pltpu.VMEM((nc, pad(2 * plies), rows), f32),
            dma(3), dma(2), dma(2),
            dma(ns), dma(ns), dma(nc), dma(nc), dma(ns), dma(ns), dma(nc), dma(nc),
        ],
        compiler_params=pltpu.CompilerParams(collective_id=0, has_side_effects=True),
    )(
        pressure, fill_state, perm_class, perm_table,
        inlet_span.reshape(1, inlets), inlet_chord.reshape(1, inlets), inlet_rate.reshape(1, inlets),
    )


def solution(mesh):
    block = P(None, "span", "chord")
    return jax.shard_map(
        functools.partial(per_device, mesh.shape["span"], mesh.shape["chord"]),
        mesh=mesh,
        in_specs=(block, block, block, P(), P(), P(), P()),
        out_specs=block,
        check_vma=False,
    )
```

time: 97 us -> 18.1 us (0.19)
  waiting for transfers between devices: 25.4 us -> 0 us
  blocking collectives: 23.7 us -> 0 us
  starting transfers between devices: 17.6 us -> 0 us
  local copies, waits for them, and re-layouts: 18.9 us -> 1.57 us
  Pallas kernels: 0 us -> 16.4 us
  other arithmetic: 9.41 us -> 0 us
  between operations: 0.99 us -> 0.01 us
    all_to_all x4 -> x0, waiting for transfers between devices: 25.4 us -> none  [the longest x2 13.2 us: to_span(): lax.all_to_all(turned, 'span', split_axis=1, concat_axis=2, tiled=True)]
    all_to_all x3 -> x0, blocking collectives: 23.7 us -> none  [the longest x1 9.74 us: span_return(): lax.all_to_all(lines, 'span', split_axis=2, concat_axis=1, tiled=True)]
    all_to_all x4 -> x0, starting transfers between devices: 17.6 us -> none  [the longest x2 10 us: to_span(): lax.all_to_all(turned, 'span', split_axis=1, concat_axis=2, tiled=True)]
    pallas_call x0 -> x1, Pallas kernels: none -> 16.4 us  [per_device(): pl.pallas_call(functools.partial(kernel, ns, nc, plies, classes), out_sha...]
    unnamed x26 -> x1, local copies, waits for them, and re-layouts: 9.18 us -> 1.57 us
    slice x64 -> x0, local copies, waits for them, and re-layouts: 4.8 us -> none  [the longest x38 2.77 us: shift_lower(): return jnp.concatenate([padding, values[..., :-stride]], axis=-1)]
    div x38 -> x0, other arithmetic: 4.47 us -> none  [the longest x17 2.4 us: line_solve(): right_hand_side / diagonal_terms]
    all_to_all x3 -> x0, other arithmetic: 3.04 us -> none  [the longest x2 2.04 us: from_chord(): lax.all_to_all(lines, 'chord', split_axis=2, concat_axis=1, tiled=True)]
  transfers between devices with their start and end apart: 4 -> 0, of which waited for: 4 -> 0; matrix products, arithmetic and copies ran while one was open for 3% -> 0% of each run, Pallas kernels for 0% -> 0%
where the time goes in v1:
time: 18.1 us; the launch traced here: 18 us
  Pallas kernels  16.4 us (91%)
  local copies, waits for them, and re-layouts  1.57 us (9%)
    pallas_call x1, Pallas kernels, per_device(): pl.pallas_call(functools.partial(kernel, ns, nc, plies, classes), out_sha...  16.4 us
    unnamed x1, local copies, waits for them, and re-layouts  1.57 us

profile of v1, /device:TPU:0, one launch (start us, length us, event | category | flops | bytes accessed | tf_op | source)
XLA Modules:
  0.0 18.0 jit_solution(2434625311108657079)
XLA Ops:
  0.0 16.4 %shard_map.73 = f32[2,128,128]{2,1,0:T(8,128)} custom-call(f32[2,128,128]{2,1,0:T(8,128)} %pressure_hbm.1, s32[2,128,128]{2,1,0:T(8,128)} %fill_hbm.1, s32[2,128,128]{2,1,0:T(8,128)} %class_hbm.1, f32[2,8]{1,0:T(2,128)} %table_ref.1, s32[1,128]{1,0:T(1,128)} %bitcast.3, s32[1,128]{1,0:T(1,128)} %bitcast.4, f32[1,128]{1,0:T(1,128)} %bitcast.5), custom_call_target="tpu_custom_call" | custom-call | tf_op jit(solution)/shard_map/pallas_call | solution.py:323
  16.4 1.6 %copy.9 = f32[2,128,128]{2,1,0:T(8,128)} copy(f32[2,128,128]{2,1,0:T(8,128)} %shard_map.73) | data formatting | bytes 262144

commit v2 on v1

--- a/solution.py
+++ b/solution.py
@@ -11,6 +11,7 @@
 COUPLE = 0.3
 MESH = pl.DeviceIdType.MESH
 TILE = 8
+LIMIT = 16 << 20
 
 
 def down(x, s):
@@ -152,9 +153,9 @@
 
 def kernel(
     ns, nc, plies, classes,
-    pressure_hbm, fill_hbm, class_hbm, table_ref, span_ref, chord_ref, rate_ref,
+    pressure_hbm, fill_hbm, class_hbm, table_hbm, span_hbm, chord_hbm, rate_hbm,
     out_ref,
-    pressure, fill, klass, half, keep_s, keep_c, A_s, C_s, E_s, A_c, C_c, E_c, D,
+    pressure, fill, klass, table_ref, span_ref, chord_ref, rate_ref, half, keep_s, keep_c, A_s, C_s, E_s, A_c, C_c, E_c, D,
     halo_out, halo_in, coef_s, coef_c, edge_s, edge_c,
     load_sem, halo_send, halo_recv,
     cs_send, cs_recv, cc_send, cc_recv, es_send, es_recv, ec_send, ec_recv,
@@ -173,20 +174,14 @@
     loads = [
         pltpu.make_async_copy(src, dst, load_sem.at[i])
         for i, (src, dst) in enumerate(
-            ((class_hbm, klass), (fill_hbm, fill), (pressure_hbm, pressure))
+            (
+                (class_hbm, klass), (fill_hbm, fill), (pressure_hbm, pressure), (table_hbm, table_ref),
+                (span_hbm, span_ref), (chord_hbm, chord_ref), (rate_hbm, rate_ref),
+            )
         )
     ]
     for load in loads:
         load.start()
-
-    row_id = lax.broadcasted_iota(jnp.int32, (rows, span_ref.shape[1]), 0) + me_s * rows
-    col_id = lax.broadcasted_iota(jnp.int32, (width, span_ref.shape[1]), 0) + me_c * width
-    row_hits = jnp.where(row_id == span_ref[...], rate_ref[...], 0.0)
-    col_hits = jnp.where(col_id == chord_ref[...], 1.0, 0.0)
-    plane = lax.dot_general(
-        row_hits, col_hits, (((1,), (1,)), ((), ())),
-        precision=lax.Precision.HIGHEST, preferred_element_type=jnp.float32,
-    )
 
     for load in loads:
         load.wait()
@@ -235,6 +230,15 @@
     span_coefs = Gather("span", ns, me_s, coef_s, cs_send, cs_recv)
     span_coefs.start()
 
+    row_id = lax.broadcasted_iota(jnp.int32, (rows, span_ref.shape[1]), 0) + me_s * rows
+    col_id = lax.broadcasted_iota(jnp.int32, (width, span_ref.shape[1]), 0) + me_c * width
+    row_hits = jnp.where(row_id == span_ref[...], rate_ref[...], 0.0)
+    col_hits = jnp.where(col_id == chord_ref[...], 1.0, 0.0)
+    plane = lax.dot_general(
+        row_hits, col_hits, (((1,), (1,)), ((), ())),
+        precision=lax.Precision.HIGHEST, preferred_element_type=jnp.float32,
+    )
+
     explicit = []
     for p in range(plies):
         f, other = fields[p], fields[plies - 1 - p]
@@ -312,37 +316,43 @@
     classes = perm_table.shape[1]
     inlets = inlet_span.shape[0]
     vmem = pl.BlockSpec(memory_space=pltpu.VMEM)
-    hbm = pl.BlockSpec(memory_space=pl.ANY)
-    smem = pl.BlockSpec(memory_space=pltpu.SMEM)
+    hbm = pl.BlockSpec(memory_space=pltpu.HBM)
     f32 = jnp.float32
     block = pltpu.VMEM((plies, rows, width), f32)
     block_t = pltpu.VMEM((plies, width, rows), f32)
     iblock = pltpu.VMEM((plies, rows, width), jnp.int32)
-    pad = lambda n: -(-n // TILE) * TILE
     dma = lambda n: pltpu.SemaphoreType.DMA((n,))
     return pl.pallas_call(
         functools.partial(kernel, ns, nc, plies, classes),
-        out_shape=jax.ShapeDtypeStruct(pressure.shape, f32),
-        in_specs=[hbm, hbm, hbm, smem, vmem, vmem, vmem],
+        out_shape=pltpu.VMEM(pressure.shape, f32),
+        in_specs=[hbm] * 7,
         out_specs=vmem,
         scratch_shapes=[
-            block, iblock, iblock, block,
+            block, iblock, iblock,
+            pltpu.SMEM(perm_table.shape, f32),
+            pltpu.VMEM((1, inlets), jnp.int32), pltpu.VMEM((1, inlets), jnp.int32), pltpu.VMEM((1, inlets), f32),
+            block,
             pltpu.VMEM((levels(rows), 2, plies, rows, width), f32),
             pltpu.VMEM((levels(width), 2, plies, width, rows), f32),
             block, block, block, block_t, block_t, block_t, block,
-            pltpu.VMEM((2, pad(2 * plies), rows), f32),
-            pltpu.VMEM((2, pad(2 * plies), rows), f32),
-            pltpu.VMEM((ns, pad(5 * plies), width), f32),
-            pltpu.VMEM((nc, pad(5 * plies), rows), f32),
-            pltpu.VMEM((ns, pad(2 * plies), width), f32),
-            pltpu.VMEM((nc, pad(2 * plies), rows), f32),
-            dma(3), dma(2), dma(2),
+            pltpu.VMEM((2, 2 * plies, rows), f32),
+            pltpu.VMEM((2, 2 * plies, rows), f32),
+            pltpu.VMEM((ns, 5 * plies, width), f32),
+            pltpu.VMEM((nc, 5 * plies, rows), f32),
+            pltpu.VMEM((ns, 2 * plies, width), f32),
+            pltpu.VMEM((nc, 2 * plies, rows), f32),
+            dma(7), dma(2), dma(2),
             dma(ns), dma(ns), dma(nc), dma(nc), dma(ns), dma(ns), dma(nc), dma(nc),
         ],
-        compiler_params=pltpu.CompilerParams(collective_id=0, has_side_effects=True),
+        compiler_params=pltpu.CompilerParams(collective_id=0, has_side_effects=True, vmem_limit_bytes=LIMIT),
     )(
-        pressure, fill_state, perm_class, perm_table,
-        inlet_span.reshape(1, inlets), inlet_chord.reshape(1, inlets), inlet_rate.reshape(1, inlets),
+        *(
+            pltpu.with_memory_space_constraint(x, pltpu.HBM)
+            for x in (
+                pressure, fill_state, perm_class, perm_table, inlet_span.reshape(1, inlets),
+                inlet_chord.reshape(1, inlets), inlet_rate.reshape(1, inlets),
+            )
+        )
     )
 
 

time: 18.1 us -> 15.7 us (0.87)
  Pallas kernels: 16.4 us -> 14.9 us
  local copies, waits for them, and re-layouts: 1.57 us -> 0.66 us
    pallas_call x1, Pallas kernels: 16.4 us -> 14.9 us  [per_device(): pl.pallas_call(functools.partial(kernel, ns, nc, plies, classes), out_sha...]
    unnamed x1, local copies, waits for them, and re-layouts: 1.57 us -> 0.66 us
where the time goes in v2:
time: 15.7 us; the launch traced here: 15.6 us
  Pallas kernels  14.9 us (95%)
  local copies, waits for them, and re-layouts  0.66 us (4%)
    pallas_call x1, Pallas kernels, per_device(): pl.pallas_call(functools.partial(kernel, ns, nc, plies, classes), out_sha...  14.9 us
    unnamed x1, local copies, waits for them, and re-layouts  0.66 us

profile of v2, /device:TPU:0, one launch (start us, length us, event | category | flops | bytes accessed | tf_op | source)
XLA Modules:
  0.0 15.6 jit_solution(13963998537407470653)
XLA Ops:
  0.0 14.9 %shard_map.73 = f32[2,128,128]{2,1,0:T(8,128)S(1)} custom-call(f32[2,128,128]{2,1,0:T(8,128)} %pressure_hbm.1, s32[2,128,128]{2,1,0:T(8,128)} %fill_hbm.1, s32[2,128,128]{2,1,0:T(8,128)} %class_hbm.1, f32[2,8]{1,0:T(2,128)} %table_hbm.1, s32[1,128]{1,0:T(1,128)} %bitcast.3, s32[1,128]{1,0:T(1,128)} %bitcast.4, f32[1,128]{1,0:T(1,128)} %bitcast.5), custom_call_target="tpu_custom_call" | custom-call | tf_op jit(solution)/shard_map/pallas_call | solution.py:325
  14.9 0.7 %copy.9 = f32[2,128,128]{2,1,0:T(8,128)} copy(f32[2,128,128]{2,1,0:T(8,128)S(1)} %shard_map.73) | data formatting | bytes 262144

commit v3 on v2

--- a/solution.py
+++ b/solution.py
@@ -155,7 +155,7 @@
     ns, nc, plies, classes,
     pressure_hbm, fill_hbm, class_hbm, table_hbm, span_hbm, chord_hbm, rate_hbm,
     out_ref,
-    pressure, fill, klass, table_ref, span_ref, chord_ref, rate_ref, half, keep_s, keep_c, A_s, C_s, E_s, A_c, C_c, E_c, D,
+    pressure, fill, klass, table_ref, span_ref, chord_ref, rate_ref, half, keep_s, keep_c, A_s, C_s, E_s, A_c, C_c, E_c, D, D_c, sides,
     halo_out, halo_in, coef_s, coef_c, edge_s, edge_c,
     load_sem, halo_send, halo_recv,
     cs_send, cs_recv, cc_send, cc_recv, es_send, es_recv, ec_send, ec_recv,
@@ -167,10 +167,6 @@
         pl.semaphore_signal(
             barrier, inc=1, device_id={"chord": lax.rem(me_c + o, nc)}, device_id_type=MESH
         )
-    for o in range(1, ns):
-        pl.semaphore_signal(
-            barrier, inc=1, device_id={"span": lax.rem(me_s + o, ns)}, device_id_type=MESH
-        )
     loads = [
         pltpu.make_async_copy(src, dst, load_sem.at[i])
         for i, (src, dst) in enumerate(
@@ -182,6 +178,10 @@
     ]
     for load in loads:
         load.start()
+    for o in range(1, ns):
+        pl.semaphore_signal(
+            barrier, inc=1, device_id={"span": lax.rem(me_s + o, ns)}, device_id_type=MESH
+        )
 
     for load in loads:
         load.wait()
@@ -247,29 +247,45 @@
         back = from_row(1, down(flow, 1), jnp.zeros_like(f))
         explicit.append(f + (flow - back) + COUPLE * (other - f))
 
+    for p in range(plies):
+        rhs = explicit[p].T + plane
+        half[p] = rhs
+        d = reduce_rhs(rhs, kept(keep_s, p), E_s[p])
+        edge_s[me_s, p : p + 1, :] = d[:1]
+        edge_s[me_s, plies + p : plies + p + 1, :] = d[rows - 1 :]
+        for q, response in enumerate((A_s[p].T, C_s[p].T)):
+            sides[2 * q, p : p + 1, :] = response[:1]
+            sides[2 * q + 1, p : p + 1, :] = response[width - 1 :]
+
     for copy in halos:
         copy.wait_recv()
-    lanes = lax.broadcasted_iota(jnp.int32, (width, rows), 0)
-    for p in range(plies):
-        behind_c, behind_f = halo_in[1, p : p + 1, :], halo_in[1, plies + p : plies + p + 1, :]
-        ahead_c, ahead_f = halo_in[0, p : p + 1, :], halo_in[0, plies + p : plies + p + 1, :]
-        first = HALF_RATE * (behind_c + turned[p][:1]) * (behind_f - fields[p][:1])
-        last = HALF_RATE * (ahead_c + turned[p][width - 1 :]) * (ahead_f - fields[p][width - 1 :])
-        first = jnp.where(me_c > 0, first, 0.0)
-        last = jnp.where(me_c < nc - 1, last, 0.0)
-        total = (
-            explicit[p]
-            + jnp.where(lanes == 0, first, 0.0)
-            + jnp.where(lanes == width - 1, last, 0.0)
-        )
-        rhs = total.T + plane
-        half[p] = rhs
-        d = reduce_rhs(rhs, kept(keep_s, p), E_s[p])
-        D[p] = d
-        edge_s[me_s, p : p + 1, :] = d[:1]
-        edge_s[me_s, plies + p : plies + p + 1, :] = d[rows - 1 :]
+
+    def inflow(mine, theirs):
+        conds_sum = halo_in[theirs, :plies, :] + halo_out[mine, :plies, :]
+        return HALF_RATE * conds_sum * (halo_in[theirs, plies:, :] - halo_out[mine, plies:, :])
+
+    first = jnp.where(me_c > 0, inflow(0, 1), 0.0)
+    last = jnp.where(me_c < nc - 1, inflow(1, 0), 0.0)
+    lane = lax.broadcasted_iota(jnp.int32, (plies, width), 1)
+    for q in range(2):
+        by_first = jnp.sum(sides[2 * q] * first, axis=1, keepdims=True)
+        by_last = jnp.sum(sides[2 * q + 1] * last, axis=1, keepdims=True)
+        edge_s[me_s, q * plies : (q + 1) * plies, :] = (
+            edge_s[me_s, q * plies : (q + 1) * plies, :]
+            + jnp.where(lane == 0, by_first, 0.0)
+            + jnp.where(lane == width - 1, by_last, 0.0)
+        )
     span_edges = Gather("span", ns, me_s, edge_s, es_send, es_recv)
     span_edges.start()
+
+    lanes = lax.broadcasted_iota(jnp.int32, (width, rows), 0)
+    for p in range(plies):
+        change = jnp.where(lanes == 0, first[p : p + 1], 0.0) + jnp.where(
+            lanes == width - 1, last[p : p + 1], 0.0
+        )
+        rhs = half[p] + change.T
+        half[p] = rhs
+        D[p] = reduce_rhs(rhs, kept(keep_s, p), E_s[p])
 
     for p in range(plies):
         A, C, re = factor(turned[p], keeper(keep_c, p))
@@ -287,7 +303,7 @@
         star, other = stars[p], stars[plies - 1 - p]
         second = 2.0 * star - half[p] + COUPLE * (other - star) + plane
         d = reduce_rhs(second.T, kept(keep_c, p), E_c[p])
-        D[p] = d
+        D_c[p] = d
         edge_c[me_c, p : p + 1, :] = d[:1]
         edge_c[me_c, plies + p : plies + p + 1, :] = d[width - 1 :]
     chord_edges = Gather("chord", nc, me_c, edge_c, ec_send, ec_recv)
@@ -298,7 +314,7 @@
     chord_edges.wait()
     top, bottom = flux_solve(edge_c, nc, plies, me_c, *parts)
     for p in range(plies):
-        line = D[p] + A_c[p] * top[p : p + 1] - C_c[p] * bottom[p : p + 1]
+        line = D_c[p] + A_c[p] * top[p : p + 1] - C_c[p] * bottom[p : p + 1]
         out_ref[p] = line.T
 
     for copy in halos:
@@ -334,7 +350,8 @@
             block,
             pltpu.VMEM((levels(rows), 2, plies, rows, width), f32),
             pltpu.VMEM((levels(width), 2, plies, width, rows), f32),
-            block, block, block, block_t, block_t, block_t, block,
+            block, block, block, block_t, block_t, block_t, block, block_t,
+            pltpu.VMEM((4, plies, rows), f32),
             pltpu.VMEM((2, 2 * plies, rows), f32),
             pltpu.VMEM((2, 2 * plies, rows), f32),
             pltpu.VMEM((ns, 5 * plies, width), f32),

time: 15.7 us -> 15.5 us (0.987)
  Pallas kernels: 14.9 us -> 14.7 us
    pallas_call x1, Pallas kernels: 14.9 us -> 14.7 us  [per_device(): pl.pallas_call(functools.partial(kernel, ns, nc, plies, classes), out_sha...]
where the time goes in v3:
time: 15.5 us; the launch traced here: 15.4 us
  Pallas kernels  14.7 us (95%)
  local copies, waits for them, and re-layouts  0.66 us (4%)
    pallas_call x1, Pallas kernels, per_device(): pl.pallas_call(functools.partial(kernel, ns, nc, plies, classes), out_sha...  14.7 us
    unnamed x1, local copies, waits for them, and re-layouts  0.66 us

profile of v3, /device:TPU:0, one launch (start us, length us, event | category | flops | bytes accessed | tf_op | source)
XLA Modules:
  0.0 15.4 jit_solution(10590870973907714317)
XLA Ops:
  0.0 14.7 %shard_map.73 = f32[2,128,128]{2,1,0:T(8,128)S(1)} custom-call(f32[2,128,128]{2,1,0:T(8,128)} %pressure_hbm.1, s32[2,128,128]{2,1,0:T(8,128)} %fill_hbm.1, s32[2,128,128]{2,1,0:T(8,128)} %class_hbm.1, f32[2,8]{1,0:T(2,128)} %table_hbm.1, s32[1,128]{1,0:T(1,128)} %bitcast.3, s32[1,128]{1,0:T(1,128)} %bitcast.4, f32[1,128]{1,0:T(1,128)} %bitcast.5), custom_call_target="tpu_custom_call" | custom-call | tf_op jit(solution)/shard_map/pallas_call | solution.py:341
  14.7 0.7 %copy.9 = f32[2,128,128]{2,1,0:T(8,128)} copy(f32[2,128,128]{2,1,0:T(8,128)S(1)} %shard_map.73) | data formatting | bytes 262144

commit v4 on v3

--- a/solution.py
+++ b/solution.py
@@ -154,8 +154,8 @@
 def kernel(
     ns, nc, plies, classes,
     pressure_hbm, fill_hbm, class_hbm, table_hbm, span_hbm, chord_hbm, rate_hbm,
-    out_ref,
-    pressure, fill, klass, table_ref, span_ref, chord_ref, rate_ref, half, keep_s, keep_c, A_s, C_s, E_s, A_c, C_c, E_c, D, D_c, sides,
+    D_c, A_c, C_c, flux_ref,
+    pressure, fill, klass, table_ref, span_ref, chord_ref, rate_ref, half, keep_s, keep_c, A_s, C_s, E_s, E_c, D, sides,
     halo_out, halo_in, coef_s, coef_c, edge_s, edge_c,
     load_sem, halo_send, halo_recv,
     cs_send, cs_recv, cc_send, cc_recv, es_send, es_recv, ec_send, ec_recv,
@@ -311,16 +311,24 @@
 
     chord_coefs.wait()
     parts = flux_factor(coef_c, nc, plies)
-    chord_edges.wait()
-    top, bottom = flux_solve(edge_c, nc, plies, me_c, *parts)
-    for p in range(plies):
-        line = D_c[p] + A_c[p] * top[p : p + 1] - C_c[p] * bottom[p : p + 1]
-        out_ref[p] = line.T
-
     for copy in halos:
         copy.wait_send()
-    for gather in (span_coefs, chord_coefs, span_edges, chord_edges):
+    for gather in (span_coefs, chord_coefs, span_edges):
         gather.wait_sent()
+    chord_edges.wait()
+    flux_ref[0], flux_ref[1] = flux_solve(edge_c, nc, plies, me_c, *parts)
+    chord_edges.wait_sent()
+
+
+def finish(plies, D_c, A_c, C_c, flux_ref, out_hbm, block, sem):
+    copies = []
+    for p in range(plies):
+        top, bottom = flux_ref[0, p : p + 1, :], flux_ref[1, p : p + 1, :]
+        block[p] = (D_c[p] + A_c[p] * top - C_c[p] * bottom).T
+        copies.append(pltpu.make_async_copy(block.at[p], out_hbm.at[p], sem.at[p]))
+        copies[-1].start()
+    for copy in copies:
+        copy.wait()
 
 
 def levels(n):
@@ -338,11 +346,12 @@
     block_t = pltpu.VMEM((plies, width, rows), f32)
     iblock = pltpu.VMEM((plies, rows, width), jnp.int32)
     dma = lambda n: pltpu.SemaphoreType.DMA((n,))
-    return pl.pallas_call(
+    lines = pltpu.VMEM((plies, width, rows), f32)
+    solved = pl.pallas_call(
         functools.partial(kernel, ns, nc, plies, classes),
-        out_shape=pltpu.VMEM(pressure.shape, f32),
+        out_shape=(lines, lines, lines, pltpu.VMEM((2, plies, rows), f32)),
         in_specs=[hbm] * 7,
-        out_specs=vmem,
+        out_specs=(vmem,) * 4,
         scratch_shapes=[
             block, iblock, iblock,
             pltpu.SMEM(perm_table.shape, f32),
@@ -350,7 +359,7 @@
             block,
             pltpu.VMEM((levels(rows), 2, plies, rows, width), f32),
             pltpu.VMEM((levels(width), 2, plies, width, rows), f32),
-            block, block, block, block_t, block_t, block_t, block, block_t,
+            block, block, block, block_t, block,
             pltpu.VMEM((4, plies, rows), f32),
             pltpu.VMEM((2, 2 * plies, rows), f32),
             pltpu.VMEM((2, 2 * plies, rows), f32),
@@ -371,6 +380,14 @@
             )
         )
     )
+    return pl.pallas_call(
+        functools.partial(finish, plies),
+        out_shape=jax.ShapeDtypeStruct(pressure.shape, f32),
+        in_specs=[vmem] * 4,
+        out_specs=hbm,
+        scratch_shapes=[block, dma(plies)],
+        compiler_params=pltpu.CompilerParams(vmem_limit_bytes=LIMIT),
+    )(*solved)
 
 
 def solution(mesh):

time: 15.5 us -> 15.5 us (level)
  Pallas kernels: 14.7 us -> 15.4 us
  local copies, waits for them, and re-layouts: 0.66 us -> 0 us
    pallas_call x0 -> x1, Pallas kernels: none -> 0.78 us  [per_device(): pl.pallas_call(functools.partial(finish, plies), out_shape=jax.ShapeDtype...]
    unnamed x1 -> x0, local copies, waits for them, and re-layouts: 0.66 us -> none
where the time goes in v4:
time: 15.5 us; the launch traced here: 15.4 us
  Pallas kernels  15.4 us (99%)
    pallas_call x1, Pallas kernels, per_device(): pl.pallas_call(functools.partial(kernel, ns, nc, plies, classes), out_sha...  14.6 us
    pallas_call x1, Pallas kernels, per_device(): pl.pallas_call(functools.partial(finish, plies), out_shape=jax.ShapeDtype...  0.78 us

profile of v4, /device:TPU:0, one launch (start us, length us, event | category | flops | bytes accessed | tf_op | source)
XLA Modules:
  0.0 15.4 jit_solution(15144465632626264933)
XLA Ops:
  0.0 14.6 %shard_map.73 = (f32[2,128,128]{2,1,0:T(8,128)S(1)}, f32[2,128,128]{2,1,0:T(8,128)S(1)}, f32[2,128,128]{2,1,0:T(8,128)S(1)}, f32[2,2,128]{2,1,0:T(2,128)S(1)}) custom-call(f32[2,128,128]{2,1,0:T(8,128)} %pressure_hbm.1, s32[2,128,128]{2,1,0:T(8,128)} %fill_hbm.1, s32[2,128,128]{2,1,0:T(8,128)} %class_hbm.1, f32[2,8]{1,0:T(2,128)} %table_hbm.1, ...), custom_call_target="tpu_custom_call" | custom-call | tf_op jit(solution)/shard_map/pallas_call | solution.py:350
  14.6 0.8 %shard_map.74 = f32[2,128,128]{2,1,0:T(8,128)} custom-call(f32[2,128,128]{2,1,0:T(8,128)S(1)} %get-tuple-element.9.D_c, f32[2,128,128]{2,1,0:T(8,128)S(1)} %get-tuple-element.10.A_c, f32[2,128,128]{2,1,0:T(8,128)S(1)} %get-tuple-element.11.C_c, f32[2,2,128]{2,1,0:T(2,128)S(1)} %get-tuple-element.12.flux_ref), custom_call_target="tpu_custom_call" | custom-call | tf_op jit(solution)/shard_map/pallas_call | solution.py:383

commit v5 on v4

--- a/solution.py
+++ b/solution.py
@@ -183,8 +183,8 @@
             barrier, inc=1, device_id={"span": lax.rem(me_s + o, ns)}, device_id_type=MESH
         )
 
-    for load in loads:
-        load.wait()
+    for i in (0, 1, 3):
+        loads[i].wait()
 
     conds, turned, fields = [], [], []
     for p in range(plies):
@@ -196,6 +196,8 @@
         cond = perm * jnp.where(st == 0, 1.0, jnp.where(st == 1, 0.5, 0.25))
         conds.append(cond)
         turned.append(cond.T)
+        if p == 0:
+            loads[2].wait()
         fields.append(pressure[p].T)
         for side, at in ((0, 0), (1, width - 1)):
             halo_out[side, p : p + 1, :] = turned[p][at : at + 1]
@@ -230,6 +232,8 @@
     span_coefs = Gather("span", ns, me_s, coef_s, cs_send, cs_recv)
     span_coefs.start()
 
+    for load in loads[4:]:
+        load.wait()
     row_id = lax.broadcasted_iota(jnp.int32, (rows, span_ref.shape[1]), 0) + me_s * rows
     col_id = lax.broadcasted_iota(jnp.int32, (width, span_ref.shape[1]), 0) + me_c * width
     row_hits = jnp.where(row_id == span_ref[...], rate_ref[...], 0.0)

time: 15.5 us -> 15.5 us (level)
  no operation moved by 1% of the time
where the time goes in v5:
time: 15.5 us; the launch traced here: 15.4 us
  Pallas kernels  15.4 us (99%)
    pallas_call x1, Pallas kernels, per_device(): pl.pallas_call(functools.partial(kernel, ns, nc, plies, classes), out_sha...  14.6 us
    pallas_call x1, Pallas kernels, per_device(): pl.pallas_call(functools.partial(finish, plies), out_shape=jax.ShapeDtype...  0.78 us

profile of v5, /device:TPU:0, one launch (start us, length us, event | category | flops | bytes accessed | tf_op | source)
XLA Modules:
  0.0 15.4 jit_solution(8638331664366136768)
XLA Ops:
  0.0 14.6 %shard_map.73 = (f32[2,128,128]{2,1,0:T(8,128)S(1)}, f32[2,128,128]{2,1,0:T(8,128)S(1)}, f32[2,128,128]{2,1,0:T(8,128)S(1)}, f32[2,2,128]{2,1,0:T(2,128)S(1)}) custom-call(f32[2,128,128]{2,1,0:T(8,128)} %pressure_hbm.1, s32[2,128,128]{2,1,0:T(8,128)} %fill_hbm.1, s32[2,128,128]{2,1,0:T(8,128)} %class_hbm.1, f32[2,8]{1,0:T(2,128)} %table_hbm.1, ...), custom_call_target="tpu_custom_call" | custom-call | tf_op jit(solution)/shard_map/pallas_call | solution.py:354
  14.6 0.8 %shard_map.74 = f32[2,128,128]{2,1,0:T(8,128)} custom-call(f32[2,128,128]{2,1,0:T(8,128)S(1)} %get-tuple-element.9.D_c, f32[2,128,128]{2,1,0:T(8,128)S(1)} %get-tuple-element.10.A_c, f32[2,128,128]{2,1,0:T(8,128)S(1)} %get-tuple-element.11.C_c, f32[2,2,128]{2,1,0:T(2,128)S(1)} %get-tuple-element.12.flux_ref), custom_call_target="tpu_custom_call" | custom-call | tf_op jit(solution)/shard_map/pallas_call | solution.py:387
